TPU v7x, 32 devices: a whole 2x2x4 slice. The times are simulated.
32 devices in a mesh: tm: 16 (over z, y, core), head: 2 (over x).
Axes of the slice: x: 2, y: 2, z: 4, core: 2. Of those that a mesh axis runs over, the one named last changes fastest.
Arguments:
- codes: int32 [16384, 8], P('tm'), may hold values from 0 to 1023
- tables: bfloat16 [8, 1024, 2048], P(None, None, 'head'), may hold values from -2.5 to 2.5
- conv_weight: bfloat16 [5, 2048, 2048], P(None, 'head'), may hold values from -0.0625 to 0.0625
- norm_gain: float32 [2048], replicated, may hold values from 0.1 to 1.9
- key_weight: bfloat16 [2048, 2048], P(None, 'head')
- value_weight: bfloat16 [2048, 2048], P(None, 'head'), may hold values from -0.125 to 0.125
- query_weight: bfloat16 [2048, 2048], P(None, 'head')
- latent_pos: int32 [512], replicated, may hold values from 0 to 4095, as said below
Outputs:
- attended: bfloat16 [512, 2048], P('tm', 'head')
Inputs may be any that keep to these rules, and one draw needn't show every extreme that they name: `latent_pos`: strictly increasing; holds every multiple of 256 and the last row 4095.
All inputs are finite; a program needn't handle non-finite values.
Results may differ from a plain program's by a relative error of at most 0.04.
The roundings to bfloat16 on the way count: a program that leaves them out, or rounds other values in their place, can miss the bound.
Values may be sent and summed in bfloat16 or wider, within the bound.
No kernel may reach another device: no remote copies, remote signals or barrier semaphores. Data moves between devices by JAX's collectives and lax.ppermute only.
A program may use at most 128 MiB of HBM per device.

v0:
```python
import math
import jax
import jax.numpy as jnp
from jax import lax
from jax.sharding import PartitionSpec as P

D = 2048
HEAD_DIM = 128
STRIDE = 4


def passed_along(value, axis, steps):
    count = lax.axis_size(axis)
    leading, last = (max(0, -steps), min(count, count - steps))
    return lax.ppermute(value, axis, [(source, source + steps) for source in range(leading, last)])


def on_device(
    codes, tables, conv_weight, norm_gain, key_weight, value_weight, query_weight, latent_pos
):
    frame_count = codes.shape[0]
    local_width = tables.shape[2]
    summed = jnp.zeros((frame_count, local_width), jnp.float32)
    for codebook in range(codes.shape[1]):
        summed = summed + jnp.take(tables[codebook], codes[:, codebook], axis=0).astype(jnp.float32)
    frames = summed.astype(jnp.bfloat16)
    taps = conv_weight.shape[0]
    lag_rows = taps - STRIDE
    row_count = frame_count // STRIDE
    previous = passed_along(frames[frame_count - lag_rows :], "tm", 1)
    padded = jnp.concatenate([previous, frames], 0)
    earlier = (
        padded[:frame_count]
        .reshape(row_count, STRIDE, local_width)[:, :lag_rows]
        .reshape(row_count, lag_rows * local_width)
    )
    latter = frames.reshape(row_count, STRIDE * local_width)
    window = jnp.concatenate([earlier, latter], 1)
    partial_value = jnp.dot(
        window,
        conv_weight.reshape(taps * local_width, conv_weight.shape[2]),
        preferred_element_type=jnp.float32,
    )
    portion = lax.psum_scatter(partial_value, "head", scatter_dimension=1, tiled=True).astype(
        jnp.bfloat16
    )
    widened = lax.all_gather(portion, "head", axis=1, tiled=True).astype(jnp.float32)
    scaled = (widened * norm_gain[None, :]).astype(jnp.bfloat16)
    key_acc = jnp.dot(scaled, key_weight, preferred_element_type=jnp.float32)
    value_acc = jnp.dot(scaled, value_weight, preferred_element_type=jnp.float32)
    query_acc = jnp.dot(scaled, query_weight, preferred_element_type=jnp.float32)
    squares = jnp.sum(widened * widened, 1)
    inverse = lax.rsqrt(squares / D + 1e-06)
    key_rows = (inverse[:, None] * key_acc).astype(jnp.bfloat16)
    value_rows = (inverse[:, None] * value_acc).astype(jnp.bfloat16)
    query_rows = (inverse[:, None] * query_acc).astype(jnp.bfloat16)
    first_row = lax.axis_index("tm") * row_count
    positions = first_row + jnp.arange(row_count, dtype=jnp.int32)
    selector = (latent_pos[:, None] == positions[None, :]).astype(jnp.bfloat16)
    selected = jnp.dot(selector, query_rows, preferred_element_type=jnp.float32)
    queries = lax.psum(selected.astype(jnp.bfloat16), "tm")
    latent_count = latent_pos.shape[0]
    group_heads = key_weight.shape[1] // HEAD_DIM
    query_three = queries.reshape(latent_count, group_heads, HEAD_DIM)
    key_three = key_rows.reshape(row_count, group_heads, HEAD_DIM)
    value_three = value_rows.reshape(row_count, group_heads, HEAD_DIM)
    scores = jnp.einsum(
        "lhd,rhd->hlr", query_three, key_three, preferred_element_type=jnp.float32
    ) * (1.0 / math.sqrt(HEAD_DIM))
    visible = (positions[None, :] <= latent_pos[:, None])[None, :, :]
    scores = jnp.where(visible, scores, -1e30)
    largest = jnp.max(scores, 2)
    weights = jnp.exp(scores - largest[:, :, None]) * visible.astype(jnp.float32)
    row_sums = jnp.sum(weights, 2)
    product = jnp.einsum(
        "hlr,rhd->lhd",
        weights.astype(jnp.bfloat16),
        value_three,
        preferred_element_type=jnp.float32,
    )
    product = product.reshape(latent_count, group_heads * HEAD_DIM)
    peaks = largest.T
    totals = row_sums.T
    peak_all = lax.pmax(peaks, "tm")
    factor = jnp.exp(peaks - peak_all)
    rescaled = product * jnp.repeat(factor, HEAD_DIM, axis=1)
    output_mine, total_mine = (
        lax.psum_scatter(
            rescaled.astype(jnp.bfloat16), "tm", scatter_dimension=0, tiled=True
        ).astype(jnp.float32),
        lax.psum_scatter(
            (totals * factor).astype(jnp.bfloat16), "tm", scatter_dimension=0, tiled=True
        ).astype(jnp.float32),
    )
    return (output_mine / jnp.repeat(total_mine, HEAD_DIM, axis=1)).astype(jnp.bfloat16)


def solution(mesh):
    placed = (
        P("tm", None),
        P(None, None, "head"),
        P(None, "head", None),
        P(),
        P(None, "head"),
        P(None, "head"),
        P(None, "head"),
        P(),
    )
    return jax.shard_map(
        on_device, mesh=mesh, in_specs=placed, out_specs=P("tm", "head"), check_vma=False
    )
```

profile of v0, /device:TPU:0, one launch (start us, length us, event | category | flops | bytes accessed | tf_op | source)
XLA Modules:
  0.0 457.3 jit_solution(12597088900499182918)
XLA Ops:
  6.5 0.0 reduce-scatter.6.cloned.1.call-start
  6.5 1.1 fusion.50
  7.8 11.5 %slice_bitcast_fusion.7 = (bf16[1024,1024]{1,0:T(8,128)(2,1)}, bf16[1024,1024]{1,0:T(8,128)(2,1)}, bf16[1024,1024]{1,0:T(8,128)(2,1)}, bf16[1024,1024]{1,0:T(8,1...) fusion(bf16[8,1024,1024]{2,1,0:T(8,128)(2,1)} %param.11), kind=kLoop, calls=%fused_computation.37 | loop fusion | bytes 33554432 | tf_op jit(solution)/shard_map/squeeze | solution.py:25
  19.2 7.9 %gather_fusion.2 = bf16[1024,1024]{1,0:T(8,128)(2,1)} fusion(bf16[1024,1024]{1,0:T(8,128)(2,1)} %get-tuple-element.12, s32[1024]{0:T(1024)S(1)} %fusion.40), kind=kCustom, calls=%fused_computation.2.clone | custom fusion | bytes 4198400 | tf_op jit(solution)/shard_map/jit(_take)/gather | solution.py:25
  27.1 7.9 %gather_fusion.3 = bf16[1024,1024]{1,0:T(8,128)(2,1)} fusion(bf16[1024,1024]{1,0:T(8,128)(2,1)} %get-tuple-element.11, s32[1024]{0:T(1024)S(1)} %fusion.41), kind=kCustom, calls=%fused_computation.3.clone | custom fusion | bytes 4198400 | tf_op jit(solution)/shard_map/jit(_take)/gather | solution.py:25
  35.0 7.9 %gather_fusion.4 = bf16[1024,1024]{1,0:T(8,128)(2,1)} fusion(bf16[1024,1024]{1,0:T(8,128)(2,1)} %get-tuple-element.10, s32[1024]{0:T(1024)S(1)} %fusion.42), kind=kCustom, calls=%fused_computation.4.clone | custom fusion | bytes 4198400 | tf_op jit(solution)/shard_map/jit(_take)/gather | solution.py:25
  42.9 7.9 %gather_fusion.5 = bf16[1024,1024]{1,0:T(8,128)(2,1)} fusion(bf16[1024,1024]{1,0:T(8,128)(2,1)} %get-tuple-element.9, s32[1024]{0:T(1024)S(1)} %fusion.43), kind=kCustom, calls=%fused_computation.5.clone | custom fusion | bytes 4198400 | tf_op jit(solution)/shard_map/jit(_take)/gather | solution.py:25
  50.8 7.9 %gather_fusion.6 = bf16[1024,1024]{1,0:T(8,128)(2,1)} fusion(bf16[1024,1024]{1,0:T(8,128)(2,1)} %get-tuple-element.15, s32[1024]{0:T(1024)S(1)} %fusion.44), kind=kCustom, calls=%fused_computation.6.clone | custom fusion | bytes 4198400 | tf_op jit(solution)/shard_map/jit(_take)/gather | solution.py:25
  58.7 7.9 %gather_fusion.7 = bf16[1024,1024]{1,0:T(8,128)(2,1)} fusion(bf16[1024,1024]{1,0:T(8,128)(2,1)} %get-tuple-element.14, s32[1024]{0:T(1024)S(1)} %fusion.45), kind=kCustom, calls=%fused_computation.7.clone | custom fusion | bytes 4198400 | tf_op jit(solution)/shard_map/jit(_take)/gather | solution.py:25
  66.5 7.9 %gather_fusion = bf16[1024,1024]{1,0:T(8,128)(2,1)} fusion(bf16[1024,1024]{1,0:T(8,128)(2,1)} %get-tuple-element.8, s32[1024]{0:T(1024)S(1)} %fusion.38), kind=kCustom, calls=%fused_computation.clone | custom fusion | bytes 4198400 | tf_op jit(solution)/shard_map/jit(_take)/gather | solution.py:25
  74.4 5.3 %gather_fusion.1 = bf16[1024,1024]{1,0:T(8,128)(2,1)} fusion(bf16[1024,1024]{1,0:T(8,128)(2,1)S(1)} %get-tuple-element.13, s32[1024]{0:T(1024)S(1)} %fusion.39), kind=kCustom, calls=%fused_computation.1.clone | custom fusion | bytes 4198400 | tf_op jit(solution)/shard_map/jit(_take)/gather | solution.py:25
  79.8 8.3 %add_convert_fusion = bf16[1024,1024]{1,0:T(8,128)(2,1)S(1)} fusion(bf16[1024,1024]{1,0:T(8,128)(2,1)} %gather_fusion.7, bf16[1024,1024]{1,0:T(8,128)(2,1)} %gather_fusion.6, bf16[1024,1024]{1,0:T(8,128)(2,1)} %gather_fusion.5, bf16[1024,1024]{1,0:T(8,128)(2,1)} %gather_fusion.4, bf16[1024,1024]{1,0:T(8,128)(2,1)} %gather_fusion.3, ...), kind=kLoop, calls=%fused_computation.10 | loop fusion | flops 25165824 | bytes 18882560 | tf_op jit(solution)/shard_map/convert_element_type | solution.py:26
  88.1 2.6 collective-permute-start
  90.6 2.6 reshape.99
  93.2 0.0 collective-permute-done
  93.2 1.9 pad_maximum_fusion
  95.1 2.7 reshape.97
  97.8 0.0 copy-start
  97.8 0.7 slice.93
  98.6 0.2 copy.41
  98.7 0.7 copy-done
  99.4 11.2 %fusion.3 = f32[256,2048]{1,0:T(8,128)} fusion(bf16[5120,2048]{1,0:T(8,128)(2,1)} %bitcast.87, bf16[256,4096]{1,0:T(8,128)(2,1)S(1)} %copy-done, bf16[256,1024]{1,0:T(8,128)(2,1)S(1)} %bitcast.67), kind=kOutput, calls=%fused_computation.16 | convolution fusion | flops 5373952000 | bytes 25690112 | tf_op jit(solution)/shard_map/dot_general | solution.py:39
  110.7 0.0 copy-start.2
  110.7 0.0 reduce-scatter.6.cloned.1.call-update
  110.7 0.0 copy-start.3
  110.7 0.0 all-gather.2.cloned.1.call-start
  110.7 34.5 %reduce-scatter.6.cloned.1.call-done = f32[256,1024]{1,0:T(8,128)} async-done(((f32[256,2048]{1,0:T(8,128)}), f32[256,1024]{1,0:T(8,128)}) %reduce-scatter.6.cloned.1.call-update) | async-done | bytes 1048592 | tf_op jit(solution)/shard_map/reduce_scatter | solution.py:44
  145.3 2.1 convert_element_type.87
  147.4 0.0 all-gather.2.cloned.1.call-update
  147.4 0.0 all-reduce.2.cloned.1.call-start
  147.5 0.0 copy-done.2
  147.5 0.2 broadcast_compare_fusion
  147.7 21.2 %all-gather.2.cloned.1.call-done = bf16[256,2048]{1,0:T(8,128)(2,1)} async-done(((bf16[256,1024]{1,0:T(8,128)(2,1)}), bf16[256,2048]{1,0:T(8,128)(2,1)}) %all-gather.2.cloned.1.call-update) | async-done | bytes 1048592 | tf_op jit(solution)/shard_map/all_gather | solution.py:47
  168.9 1.5 fusion.7
  170.4 0.0 copy-done.3
  170.4 4.0 fusion.19
  174.4 0.0 copy-start.1
  174.5 1.2 copy.40
  175.7 0.0 all-reduce.2.cloned.1.call-update
  175.7 0.0 reduce-scatter.10.cloned.1.call-start
  175.7 0.2 copy-done.1
  175.9 3.4 fusion.20
  179.4 0.2 copy.24
  179.6 3.6 fusion.23
  183.1 86.5 %all-reduce.2.cloned.1.call-done = bf16[512,8,128]{2,0,1:T(8,128)(2,1)} async-done(((bf16[512,8,128]{2,0,1:T(8,128)(2,1)}), bf16[512,8,128]{2,0,1:T(8,128)(2,1)}) %all-reduce.2.cloned.1.call-update) | async-done | bytes 1048592 | tf_op jit(solution)/shard_map/psum | solution.py:61
  269.7 4.0 fusion
  273.7 58.4 %pmax.7 = f32[512,8]{0,1:T(8,128)S(1)} all-reduce(f32[512,8]{0,1:T(8,128)S(1)} %bitcast.70), channel_id=1, replica_groups=mesh['tm'=16,'head'=2] {'tm'}, use_global_device_ids=true, to_apply=%region_4.6 | all-reduce | flops 4096 | bytes 32768 | tf_op jit(solution)/shard_map/pmax | solution.py:84
  332.1 3.2 fusion.1
  335.3 0.8 copy.25
  336.1 0.0 reduce-scatter.10.cloned.1.call-update
  336.1 0.0 reduce-scatter.8.cloned.1.call-start
  336.2 3.6 fusion.11
  339.8 1.3 copy.21
  341.1 0.0 reduce-scatter.8.cloned.1.call-update
  341.1 48.0 %reduce-scatter.10.cloned.1.call-done = bf16[32,8]{1,0:T(8,128)(2,1)} async-done(((bf16[512,8]{1,0:T(8,128)(2,1)}), bf16[32,8]{1,0:T(8,128)(2,1)}) %reduce-scatter.10.cloned.1.call-update) | async-done | bytes 528
  389.2 0.8 copy.26
  389.9 0.1 copy.22
  390.0 59.2 %reduce-scatter.8.cloned.1.call-done = bf16[32,1024]{1,0:T(8,128)(2,1)} async-done(((bf16[512,1024]{1,0:T(8,128)(2,1)}), bf16[32,1024]{1,0:T(8,128)(2,1)}) %reduce-scatter.8.cloned.1.call-update) | async-done | bytes 65552 | tf_op jit(solution)/shard_map/reduce_scatter | solution.py:88
  449.2 0.1 broadcast_in_dim.40
  449.3 1.5 fusion.36
  (16 shorter events, 0.1 us)
Async XLA Ops:
  6.5 138.8 %reduce-scatter.6.cloned.1.call-start = ((), (), s32[]{:S(2)}) async-start(), calls=%async_computation.3 | async-start | bytes 3145728 | tf_op jit(solution)/shard_map/reduce_scatter | solution.py:44
  88.1 5.1 %collective-permute-start = (bf16[1,1024]{1,0:T(2,128)(2,1)S(1)}, bf16[1,1024]{1,0:T(2,128)(2,1)S(1)}, u32[]{:S(2)}, u32[]{:S(2)}) collective-permute-start(bf16[1,1024]{1,0:T(2,128)(2,1)S(1)} %slice.92), channel_id=1, source_target_pairs={{0,2},{2,4},{4,6},{6,8},{8,10},{10,12},{12,14},{14,16},{16,18},{18... | collective-permute-start | bytes 6152 | tf_op jit(solution)/shard_map/ppermute | solution.py:15
  97.8 1.6 copy-start
  110.7 36.8 %copy-start.2 = (s32[512]{0:T(512)S(1)}, s32[512]{0:T(512)}, u32[]{:S(2)}) copy-start(s32[512]{0:T(512)} %param.17) | copy-start | bytes 6148
  110.7 59.7 %copy-start.3 = (f32[2048]{0:T(1024)S(1)}, f32[2048]{0:T(1024)}, u32[]{:S(2)}) copy-start(f32[2048]{0:T(1024)} %param.13) | copy-start | bytes 24580
  110.7 58.2 %all-gather.2.cloned.1.call-start = ((), (), s32[]{:S(2)}) async-start(), calls=%async_computation.4 | async-start | bytes 1572864 | tf_op jit(solution)/shard_map/all_gather | solution.py:47
  147.4 122.3 %all-reduce.2.cloned.1.call-start = ((), (), s32[]{:S(2)}) async-start(), calls=%async_computation.5 | async-start | bytes 2097152 | tf_op jit(solution)/shard_map/psum | solution.py:61
  174.4 1.5 copy-start.1
  175.7 213.5 %reduce-scatter.10.cloned.1.call-start = ((), (), s32[]{:S(2)}) async-start(), calls=%async_computation.7 | async-start | bytes 139264
  336.1 113.1 %reduce-scatter.8.cloned.1.call-start = ((), (), s32[]{:S(2)}) async-start(), calls=%async_computation.6 | async-start | bytes 1114112 | tf_op jit(solution)/shard_map/reduce_scatter | solution.py:88
Sparse Core Ops, SparseCore 0:
  110.8 34.4 reduce-scatter.5
  147.5 21.2 all-gather.1
  175.8 93.8 all-reduce.1
  336.2 52.8 reduce-scatter.9
  392.6 56.5 reduce-scatter.7
where the time goes:
time: 458 us; the launch traced here: 457 us
  waiting for transfers between devices  250 us (55%)
  local copies, waits for them, and re-layouts  84.5 us (18%)
  blocking collectives  58.4 us (13%)
  matrix products  29.9 us (7%)
  other arithmetic  18.7 us (4%)
  between operations  13.4 us (3%)
    psum x1, waiting for transfers between devices, on_device(): queries = lax.psum(selected.astype(jnp.bfloat16), 'tm')  86.5 us
    gather x8, local copies, waits for them, and re-layouts, on_device(): jnp.take(tables[codebook], codes[:, codebook], axis=0).astype(jnp.float32)  60.5 us
    reduce_scatter x1, waiting for transfers between devices, on_device(): lax.psum_scatter(rescaled.astype(jnp.bfloat16), 'tm', scatter_dimension=0...  59.2 us
    pmax x1, blocking collectives, on_device(): peak_all = lax.pmax(peaks, 'tm')  58.4 us
    unnamed x6, waiting for transfers between devices  48.1 us
    reduce_scatter x1, waiting for transfers between devices, on_device(): lax.psum_scatter(partial_value, 'head', scatter_dimension=1, tiled=True)  34.5 us
    all_gather x1, waiting for transfers between devices, on_device(): lax.all_gather(portion, 'head', axis=1, tiled=True).astype(jnp.float32)  21.2 us
    squeeze x1, local copies, waits for them, and re-layouts, on_device(): tables[codebook]  11.5 us
  transfers between devices with their start and end apart: 6, of which 5 were waited for; matrix products, arithmetic and copies ran while one was open for 3% of the time, Pallas kernels for 0%

commit v1 on v0

--- a/solution.py
+++ b/solution.py
@@ -58,7 +58,7 @@
     positions = first_row + jnp.arange(row_count, dtype=jnp.int32)
     selector = (latent_pos[:, None] == positions[None, :]).astype(jnp.bfloat16)
     selected = jnp.dot(selector, query_rows, preferred_element_type=jnp.float32)
-    queries = lax.psum(selected.astype(jnp.bfloat16), "tm")
+    queries = lax.all_gather(selected.astype(jnp.bfloat16), axis_name="tm").sum(axis=0)
     latent_count = latent_pos.shape[0]
     group_heads = key_weight.shape[1] // HEAD_DIM
     query_three = queries.reshape(latent_count, group_heads, HEAD_DIM)

time: 458 us -> 500 us (1.092)
  waiting for transfers between devices: 250 us -> 282 us
  other arithmetic: 18.7 us -> 28.1 us
    all_gather x0 -> x1, waiting for transfers between devices: none -> 118 us  [on_device(): lax.all_gather(selected.astype(jnp.bfloat16), axis_name='tm').sum(axis=0)]
    psum x1 -> x0, waiting for transfers between devices: 86.5 us -> none  [on_device(): queries = lax.psum(selected.astype(jnp.bfloat16), 'tm')]
    reduce_sum x0 -> x1, other arithmetic: none -> 9.33 us  [on_device(): lax.all_gather(selected.astype(jnp.bfloat16), axis_name='tm').sum(axis=0)]
where the time goes in v1:
time: 500 us; the launch traced here: 499 us
  waiting for transfers between devices  282 us (56%)
  local copies, waits for them, and re-layouts  84.7 us (17%)
  blocking collectives  58.7 us (12%)
  matrix products  29.7 us (6%)
  other arithmetic  28.1 us (6%)
  between operations  13.4 us (3%)
    all_gather x1, waiting for transfers between devices, on_device(): lax.all_gather(selected.astype(jnp.bfloat16), axis_name='tm').sum(axis=0)  118 us
    gather x8, local copies, waits for them, and re-layouts, on_device(): jnp.take(tables[codebook], codes[:, codebook], axis=0).astype(jnp.float32)  60.7 us
    reduce_scatter x1, waiting for transfers between devices, on_device(): lax.psum_scatter(rescaled.astype(jnp.bfloat16), 'tm', scatter_dimension=0...  59.3 us
    pmax x1, blocking collectives, on_device(): peak_all = lax.pmax(peaks, 'tm')  58.7 us
    unnamed x6, waiting for transfers between devices  48.1 us
    reduce_scatter x1, waiting for transfers between devices, on_device(): lax.psum_scatter(partial_value, 'head', scatter_dimension=1, tiled=True)  34.5 us
    all_gather x1, waiting for transfers between devices, on_device(): lax.all_gather(portion, 'head', axis=1, tiled=True).astype(jnp.float32)  21.4 us
    squeeze x1, local copies, waits for them, and re-layouts, on_device(): tables[codebook]  11.4 us
  transfers between devices with their start and end apart: 6, of which 5 were waited for; matrix products, arithmetic and copies ran while one was open for 3% of the time, Pallas kernels for 0%

profile of v1, /device:TPU:0, one launch (start us, length us, event | category | flops | bytes accessed | tf_op | source)
XLA Modules:
  0.0 499.2 jit_solution(15770851519805647847)
XLA Ops:
  6.5 0.0 reduce-scatter.6.cloned.1.call-start
  6.5 1.1 fusion.48
  7.8 11.4 %slice_bitcast_fusion.7 = (bf16[1024,1024]{1,0:T(8,128)(2,1)}, bf16[1024,1024]{1,0:T(8,128)(2,1)}, bf16[1024,1024]{1,0:T(8,128)(2,1)}, bf16[1024,1024]{1,0:T(8,1...) fusion(bf16[8,1024,1024]{2,1,0:T(8,128)(2,1)} %param.11), kind=kLoop, calls=%fused_computation.37 | loop fusion | bytes 33554432 | tf_op jit(solution)/shard_map/squeeze | solution.py:25
  19.2 7.9 %gather_fusion.2 = bf16[1024,1024]{1,0:T(8,128)(2,1)} fusion(bf16[1024,1024]{1,0:T(8,128)(2,1)} %get-tuple-element.12, s32[1024]{0:T(1024)S(1)} %fusion.38), kind=kCustom, calls=%fused_computation.2.clone | custom fusion | bytes 4198400 | tf_op jit(solution)/shard_map/jit(_take)/gather | solution.py:25
  27.1 7.9 %gather_fusion.3 = bf16[1024,1024]{1,0:T(8,128)(2,1)} fusion(bf16[1024,1024]{1,0:T(8,128)(2,1)} %get-tuple-element.11, s32[1024]{0:T(1024)S(1)} %fusion.39), kind=kCustom, calls=%fused_computation.3.clone | custom fusion | bytes 4198400 | tf_op jit(solution)/shard_map/jit(_take)/gather | solution.py:25
  35.0 7.9 %gather_fusion.4 = bf16[1024,1024]{1,0:T(8,128)(2,1)} fusion(bf16[1024,1024]{1,0:T(8,128)(2,1)} %get-tuple-element.10, s32[1024]{0:T(1024)S(1)} %fusion.40), kind=kCustom, calls=%fused_computation.4.clone | custom fusion | bytes 4198400 | tf_op jit(solution)/shard_map/jit(_take)/gather | solution.py:25
  42.9 7.9 %gather_fusion.5 = bf16[1024,1024]{1,0:T(8,128)(2,1)} fusion(bf16[1024,1024]{1,0:T(8,128)(2,1)} %get-tuple-element.9, s32[1024]{0:T(1024)S(1)} %fusion.41), kind=kCustom, calls=%fused_computation.5.clone | custom fusion | bytes 4198400 | tf_op jit(solution)/shard_map/jit(_take)/gather | solution.py:25
  50.8 7.9 %gather_fusion.6 = bf16[1024,1024]{1,0:T(8,128)(2,1)} fusion(bf16[1024,1024]{1,0:T(8,128)(2,1)} %get-tuple-element.15, s32[1024]{0:T(1024)S(1)} %fusion.42), kind=kCustom, calls=%fused_computation.6.clone | custom fusion | bytes 4198400 | tf_op jit(solution)/shard_map/jit(_take)/gather | solution.py:25
  58.7 7.9 %gather_fusion.7 = bf16[1024,1024]{1,0:T(8,128)(2,1)} fusion(bf16[1024,1024]{1,0:T(8,128)(2,1)} %get-tuple-element.14, s32[1024]{0:T(1024)S(1)} %fusion.43), kind=kCustom, calls=%fused_computation.7.clone | custom fusion | bytes 4198400 | tf_op jit(solution)/shard_map/jit(_take)/gather | solution.py:25
  66.6 7.9 %gather_fusion = bf16[1024,1024]{1,0:T(8,128)(2,1)} fusion(bf16[1024,1024]{1,0:T(8,128)(2,1)} %get-tuple-element.8, s32[1024]{0:T(1024)S(1)} %fusion.36), kind=kCustom, calls=%fused_computation.clone | custom fusion | bytes 4198400 | tf_op jit(solution)/shard_map/jit(_take)/gather | solution.py:25
  74.6 5.3 %gather_fusion.1 = bf16[1024,1024]{1,0:T(8,128)(2,1)} fusion(bf16[1024,1024]{1,0:T(8,128)(2,1)S(1)} %get-tuple-element.13, s32[1024]{0:T(1024)S(1)} %fusion.37), kind=kCustom, calls=%fused_computation.1.clone | custom fusion | bytes 4198400 | tf_op jit(solution)/shard_map/jit(_take)/gather | solution.py:25
  79.9 8.3 %add_convert_fusion = bf16[1024,1024]{1,0:T(8,128)(2,1)S(1)} fusion(bf16[1024,1024]{1,0:T(8,128)(2,1)} %gather_fusion.7, bf16[1024,1024]{1,0:T(8,128)(2,1)} %gather_fusion.6, bf16[1024,1024]{1,0:T(8,128)(2,1)} %gather_fusion.5, bf16[1024,1024]{1,0:T(8,128)(2,1)} %gather_fusion.4, bf16[1024,1024]{1,0:T(8,128)(2,1)} %gather_fusion.3, ...), kind=kLoop, calls=%fused_computation.10 | loop fusion | flops 25165824 | bytes 18882560 | tf_op jit(solution)/shard_map/convert_element_type | solution.py:26
  88.2 2.6 collective-permute-start
  90.8 2.6 reshape.99
  93.3 0.0 collective-permute-done
  93.4 1.9 pad_maximum_fusion
  95.2 2.7 reshape.97
  98.0 0.0 copy-start
  98.0 0.7 slice.93
  98.7 0.2 copy.46
  98.9 0.7 copy-done
  99.6 11.3 %fusion.3 = f32[256,2048]{1,0:T(8,128)} fusion(bf16[5120,2048]{1,0:T(8,128)(2,1)} %bitcast.85, bf16[256,4096]{1,0:T(8,128)(2,1)S(1)} %copy-done, bf16[256,1024]{1,0:T(8,128)(2,1)S(1)} %bitcast.65), kind=kOutput, calls=%fused_computation.16 | convolution fusion | flops 5373952000 | bytes 25690112 | tf_op jit(solution)/shard_map/dot_general | solution.py:39
  110.8 0.0 reduce-scatter.6.cloned.1.call-update
  110.9 0.0 copy-start.3
  110.9 0.0 copy-start.4
  110.9 0.0 all-gather.4.cloned.1.call-start
  110.9 34.5 %reduce-scatter.6.cloned.1.call-done = f32[256,1024]{1,0:T(8,128)} async-done(((f32[256,2048]{1,0:T(8,128)}), f32[256,1024]{1,0:T(8,128)}) %reduce-scatter.6.cloned.1.call-update) | async-done | bytes 1048592 | tf_op jit(solution)/shard_map/reduce_scatter | solution.py:44
  145.5 2.1 convert_element_type.89
  147.6 0.0 all-gather.4.cloned.1.call-update
  147.6 0.0 all-gather.6.cloned.1.call-start
  147.7 21.4 %all-gather.4.cloned.1.call-done = bf16[256,2048]{1,0:T(8,128)(2,1)} async-done(((bf16[256,1024]{1,0:T(8,128)(2,1)}), bf16[256,2048]{1,0:T(8,128)(2,1)}) %all-gather.4.cloned.1.call-update) | async-done | bytes 1048592 | tf_op jit(solution)/shard_map/all_gather | solution.py:47
  169.0 1.5 fusion.7
  170.6 0.0 copy-done.3
  170.6 0.0 copy-done.4
  170.6 0.0 copy-start.1
  170.6 5.2 %convolution_convert_fusion = bf16[512,1024]{1,0:T(8,128)(2,1)} fusion(bf16[2048,1024]{1,0:T(8,128)(2,1)} %param.16, bf16[256,2048]{1,0:T(8,128)(2,1)} %all-gather.4.cloned.1.call-done, f32[2048]{0:T(1024)S(1)} %copy-done.4, f32[256]{0:T(256)S(1)} %add_rsqrt_fusion, s32[512]{0:T(512)S(1)} %copy-done.3, s32[256]{0:T(256)S(1)} %iota_add_fusion), kind=kOutput, calls=%fused_computation.39 | convolution fusion | flops 1344929792 | bytes 6303744 | tf_op jit(solution)/shard_map/dot_general | solution.py:60
  175.8 0.0 all-gather.6.cloned.1.call-update
  175.8 0.0 reduce-scatter.10.cloned.1.call-start
  175.8 0.2 broadcast_compare_fusion
  176.0 0.0 copy-done.1
  176.0 3.4 fusion.19
  179.4 1.0 copy.32
  180.5 3.4 fusion.22
  183.9 118.5 %all-gather.6.cloned.1.call-done = bf16[8192,1024]{1,0:T(8,128)(2,1)} async-done(((bf16[512,1024]{1,0:T(8,128)(2,1)}), bf16[8192,1024]{1,0:T(8,128)(2,1)}) %all-gather.6.cloned.1.call-update) | async-done | bytes 16777232 | tf_op jit(solution)/shard_map/all_gather | solution.py:61
  302.4 9.3 %reduce_sum.31 = bf16[512,1024]{1,0:T(8,128)(2,1)S(1)} reduce(bf16[16,512,1024]{2,1,0:T(8,128)(2,1)} %bitcast.62, bf16[]{:T(256)} %constant.14.clone.1), dimensions={0}, to_apply=%region_2.4 | reduce | flops 7864320 | bytes 17825794 | tf_op jit(solution)/shard_map/reduce_sum | solution.py:61
  311.7 0.5 copy.23
  312.2 2.8 fusion
  315.1 58.7 %pmax.7 = f32[512,8]{0,1:T(8,128)S(1)} all-reduce(f32[512,8]{0,1:T(8,128)S(1)} %bitcast.68), channel_id=1, replica_groups=mesh['tm'=16,'head'=2] {'tm'}, use_global_device_ids=true, to_apply=%region_4.6 | all-reduce | flops 4096 | bytes 32768 | tf_op jit(solution)/shard_map/pmax | solution.py:84
  373.8 0.0 copy-start.2
  373.8 3.3 fusion.1
  377.0 0.8 copy.33
  377.8 0.0 reduce-scatter.10.cloned.1.call-update
  377.9 0.0 reduce-scatter.8.cloned.1.call-start
  377.9 0.0 copy-done.2
  377.9 3.6 fusion.11
  381.5 1.3 copy.28
  382.8 0.0 reduce-scatter.8.cloned.1.call-update
  382.9 48.0 %reduce-scatter.10.cloned.1.call-done = bf16[32,8]{1,0:T(8,128)(2,1)} async-done(((bf16[512,8]{1,0:T(8,128)(2,1)}), bf16[32,8]{1,0:T(8,128)(2,1)}) %reduce-scatter.10.cloned.1.call-update) | async-done | bytes 528
  430.9 0.8 copy.34
  431.7 0.1 copy.29
  431.8 59.3 %reduce-scatter.8.cloned.1.call-done = bf16[32,1024]{1,0:T(8,128)(2,1)} async-done(((bf16[512,1024]{1,0:T(8,128)(2,1)}), bf16[32,1024]{1,0:T(8,128)(2,1)}) %reduce-scatter.8.cloned.1.call-update) | async-done | bytes 65552 | tf_op jit(solution)/shard_map/reduce_scatter | solution.py:88
  491.1 0.1 broadcast_in_dim.40
  491.2 1.5 fusion.34
  (16 shorter events, 0.1 us)
Async XLA Ops:
  6.5 138.9 %reduce-scatter.6.cloned.1.call-start = ((), (), s32[]{:S(2)}) async-start(), calls=%async_computation.3 | async-start | bytes 3145728 | tf_op jit(solution)/shard_map/reduce_scatter | solution.py:44
  88.2 5.2 %collective-permute-start = (bf16[1,1024]{1,0:T(2,128)(2,1)S(1)}, bf16[1,1024]{1,0:T(2,128)(2,1)S(1)}, u32[]{:S(2)}, u32[]{:S(2)}) collective-permute-start(bf16[1,1024]{1,0:T(2,128)(2,1)S(1)} %slice.92), channel_id=1, source_target_pairs={{0,2},{2,4},{4,6},{6,8},{8,10},{10,12},{12,14},{14,16},{16,18},{18... | collective-permute-start | bytes 6152 | tf_op jit(solution)/shard_map/ppermute | solution.py:15
  98.0 1.6 copy-start
  110.9 59.7 %copy-start.3 = (s32[512]{0:T(512)S(1)}, s32[512]{0:T(512)}, u32[]{:S(2)}) copy-start(s32[512]{0:T(512)} %param.17) | copy-start | bytes 6148
  110.9 59.7 %copy-start.4 = (f32[2048]{0:T(1024)S(1)}, f32[2048]{0:T(1024)}, u32[]{:S(2)}) copy-start(f32[2048]{0:T(1024)} %param.13) | copy-start | bytes 24580
  110.9 58.2 %all-gather.4.cloned.1.call-start = ((), (), s32[]{:S(2)}) async-start(), calls=%async_computation.4 | async-start | bytes 1572864 | tf_op jit(solution)/shard_map/all_gather | solution.py:47
  147.6 154.8 %all-gather.6.cloned.1.call-start = ((), (), s32[]{:S(2)}) async-start(), calls=%async_computation.6 | async-start | bytes 17825792 | tf_op jit(solution)/shard_map/all_gather | solution.py:61
  170.6 5.4 %copy-start.1 = (bf16[256,2048]{1,0:T(8,128)(2,1)S(1)}, bf16[256,2048]{1,0:T(8,128)(2,1)}, u32[]{:S(2)}) copy-start(bf16[256,2048]{1,0:T(8,128)(2,1)} %all-gather.4.cloned.1.call-done) | copy-start | bytes 3145732
  175.8 255.1 %reduce-scatter.10.cloned.1.call-start = ((), (), s32[]{:S(2)}) async-start(), calls=%async_computation.7 | async-start | bytes 139264
  373.8 4.1 copy-start.2
  377.9 113.2 %reduce-scatter.8.cloned.1.call-start = ((), (), s32[]{:S(2)}) async-start(), calls=%async_computation.5 | async-start | bytes 1114112 | tf_op jit(solution)/shard_map/reduce_scatter | solution.py:88
Sparse Core Ops, SparseCore 0:
  111.0 34.4 reduce-scatter.5
  147.7 21.2 all-gather.3
  175.9 126.4 all-gather.5
  378.0 52.8 reduce-scatter.9
  434.4 56.6 reduce-scatter.7
